TPU v7x, 128 devices: a whole 4x4x4 slice. The times are simulated.
128 devices in a mesh: dp: 8 (over z, core), tensor: 16 (over y, x).
Axes of the slice: x: 4, y: 4, z: 4, core: 2. Of those that a mesh axis runs over, the one named last changes fastest.
Arguments:
- residues: bfloat16 [4096, 1024], P('dp'), may hold values from -40 to 40
- block_protein: int32 [32], P('dp'), may hold values from 0 to 31, as said below
- protein_length: int32 [32], replicated, may hold values from 0 to 256, as said below
- decoder_group: int32 [32], replicated, may hold values from 0 to 7, as said below
- enc_gain: float32 [1024], replicated, may hold values from 0.1 to 1.9
- enc_query: bfloat16 [1024, 16384], P(None, 'tensor'), may hold values from -2 to 2
- enc_key: bfloat16 [1024, 16384], P(None, 'tensor'), may hold values from -2 to 2
- enc_value: bfloat16 [1024, 16384], P(None, 'tensor'), may hold values from -0.1875 to 0.1875
- enc_out: bfloat16 [16384, 1024], P('tensor'), may hold values from -0.1875 to 0.1875
- decoder_states: bfloat16 [3072, 1024], P('dp'), may hold values from -40 to 40
- query_protein: int32 [3072], P('dp'), may hold values from 0 to 31, as said below
- dec_gain: float32 [1024], replicated, may hold values from 0.1 to 1.9
- final_gain: float32 [1024], replicated, may hold values from 0.1 to 1.9
- cross_query: bfloat16 [1024, 16384], P(None, 'tensor'), may hold values from -2 to 2
- cross_key: bfloat16 [1024, 16384], P(None, 'tensor'), may hold values from -2 to 2
- cross_value: bfloat16 [1024, 16384], P(None, 'tensor'), may hold values from -0.1875 to 0.1875
- cross_out: bfloat16 [16384, 1024], P('tensor'), may hold values from -0.1875 to 0.1875
Outputs:
- encoded: bfloat16 [4096, 1024], P('dp', 'tensor')
- decoded: bfloat16 [3072, 1024], P(('dp', 'tensor'))
Inputs may be any that keep to these rules, and one draw needn't show every extreme that they name: `block_protein`: block b of dp group d names a protein id from d * 4 to (d + 1) * 4 - 1; the blocks of one protein are consecutive and the ids rise along a group's blocks. `protein_length`: A protein of n blocks has a length from (n - 1) * 128 + 1 to n * 128; an id that no block names has length 0; no protein spans more than 2 blocks. `decoder_group`: at most 2 blocks of one dp group belong to proteins of one decoder group, and in every draw some decoder group gets exactly 2 blocks from every dp group; every decoder group owns a protein of positive length. `query_protein`: query row i names a protein of positive length whose decoder group is i // 384.
All inputs are finite; a program needn't handle non-finite values.
Results may differ from a plain program's by a relative error of at most 0.017.
Values may be sent and summed in bfloat16 or wider, within the bound.
No kernel may reach another device: no remote copies, remote signals or barrier semaphores. Data moves between devices by JAX's collectives and lax.ppermute only.
A program may use at most 128 MiB of HBM per device.

v0:
```python
import jax
import jax.numpy as jnp
from jax import lax
from jax.sharding import PartitionSpec as P

HEAD_DIM = 128
BLOCK = 128
EPSILON = 1e-06
MASKED = -1000000000.0


def split_up(x, dim, size):
    before, after = (x.shape[:dim], x.shape[dim + 1 :])
    return jnp.moveaxis(x.reshape(*before, size, -1, *after), dim, 0)


def sent_and_summed(x, axis, dim):
    blocks = split_up(x, dim, lax.axis_size(axis))
    arrived = lax.all_to_all(blocks, axis, split_axis=0, concat_axis=0, tiled=True)
    return arrived.sum(axis=0)


def summed_on_arrival(x, axis, dim):
    blocks = split_up(x, dim, lax.axis_size(axis))
    arrived = lax.all_to_all(blocks, axis, split_axis=0, concat_axis=0, tiled=True)
    return arrived.astype(jnp.float32).sum(axis=0)


def row_scale(matrix):
    values = matrix.astype(jnp.float32)
    return lax.rsqrt(jnp.mean(values * values, axis=1, keepdims=True) + EPSILON)


def table_lookup(indices, table):
    match = indices[:, None] == jnp.arange(table.shape[0], dtype=jnp.int32)[None, :]
    return jnp.sum(jnp.where(match, table[None, :], 0), axis=1)


def attend(queries, keys, values, allowed):
    count = queries.shape[0]
    heads = queries.shape[1] // HEAD_DIM
    query_heads = queries.reshape(count, heads, HEAD_DIM)
    key_heads = keys.reshape(keys.shape[0], heads, HEAD_DIM)
    value_heads = values.reshape(values.shape[0], heads, HEAD_DIM)
    scores = jnp.einsum(
        "qhd,khd->hqk", query_heads, key_heads, preferred_element_type=jnp.float32
    ) * HEAD_DIM ** (-0.5)
    scores = jnp.where(allowed[None], scores, MASKED)
    top = jnp.max(scores, axis=2, keepdims=True)
    expo = jnp.exp(scores - top)
    total = jnp.sum(expo, axis=2)
    weights = expo.astype(jnp.bfloat16)
    context = jnp.einsum("hqk,khd->qhd", weights, value_heads, preferred_element_type=jnp.float32)
    context = context / jnp.transpose(total)[:, :, None]
    return context.reshape(count, heads * HEAD_DIM).astype(jnp.bfloat16)


def body(
    residues,
    block_protein,
    protein_length,
    decoder_group,
    enc_gain,
    enc_query,
    enc_key,
    enc_value,
    enc_out,
    decoder_states,
    query_protein,
    dec_gain,
    final_gain,
    cross_query,
    cross_key,
    cross_value,
    cross_out,
):
    groups = lax.axis_size("dp")
    tensor_count = lax.axis_size("tensor")
    tensor_index = lax.axis_index("tensor")
    tok_rows = residues.shape[0]
    width = residues.shape[1]
    blocks = block_protein.shape[0]
    slots = blocks // 2
    order = jnp.arange(blocks, dtype=jnp.int32)
    same = block_protein[:, None] == block_protein[None, :]
    offset = jnp.sum(same & (order[None, :] < order[:, None]), axis=1)
    live = jnp.clip(table_lookup(block_protein, protein_length) - offset * BLOCK, 0, BLOCK)
    dest = table_lookup(block_protein, decoder_group)
    position = jnp.arange(BLOCK, dtype=jnp.int32)
    token_protein = jnp.broadcast_to(block_protein[:, None], (blocks, BLOCK)).reshape(tok_rows)
    token_valid = (position[None, :] < live[:, None]).reshape(tok_rows)
    normed = (residues.astype(jnp.float32) * row_scale(residues) * enc_gain[None, :]).astype(
        jnp.bfloat16
    )
    enc_queries = jnp.dot(normed, enc_query, preferred_element_type=jnp.float32).astype(
        jnp.bfloat16
    )
    enc_keys = jnp.dot(normed, enc_key, preferred_element_type=jnp.float32).astype(jnp.bfloat16)
    enc_values = jnp.dot(normed, enc_value, preferred_element_type=jnp.float32).astype(jnp.bfloat16)
    row_block = min(tok_rows, 512)
    block_count = tok_rows // row_block

    def encode_block(item):
        block_queries, block_owner = item
        permit = (block_owner[:, None] == token_protein[None, :]) & token_valid[None, :]
        return attend(block_queries, enc_keys, enc_values, permit)

    context = lax.map(
        encode_block,
        (
            enc_queries.reshape(block_count, row_block, -1),
            token_protein.reshape(block_count, row_block),
        ),
    )
    context = context.reshape(tok_rows, -1)
    partial_value = jnp.dot(context, enc_out, preferred_element_type=jnp.float32)
    slice_width = width // tensor_count
    column_start = tensor_index * slice_width
    same_dest = dest[:, None] == dest[None, :]
    rank = jnp.sum(same_dest & (order[None, :] < order[:, None]), axis=1)
    place = dest * slots + rank
    target = jnp.arange(groups * slots, dtype=jnp.int32)
    chosen = target[:, None] == place[None, :]
    occupied = jnp.any(chosen, axis=1)
    send_ids = jnp.where(
        occupied, jnp.sum(jnp.where(chosen, block_protein[None, :], 0), axis=1), -1
    )
    send_live = jnp.sum(jnp.where(chosen, live[None, :], 0), axis=1)
    send_meta = jnp.stack([send_ids, send_live], axis=-1).reshape(groups, slots, 2)
    shares = sent_and_summed(partial_value, "tensor", 1)
    own_columns = lax.dynamic_slice_in_dim(residues, column_start, slice_width, 1)
    encoded = (own_columns.astype(jnp.float32) + shares).astype(jnp.bfloat16)
    features = encoded.shape[1]
    stacked = encoded.reshape(blocks, BLOCK * features)
    placed = jnp.dot(
        chosen.astype(jnp.bfloat16), stacked, preferred_element_type=jnp.float32
    ).astype(jnp.bfloat16)
    slice_grid = lax.all_to_all(
        placed.reshape(groups, slots, BLOCK, features),
        "dp",
        split_axis=0,
        concat_axis=0,
        tiled=True,
    )
    meta = lax.all_to_all(send_meta, "dp", split_axis=0, concat_axis=0, tiled=True)
    flat = slice_grid.reshape(-1, slice_width)
    inner = cross_key.shape[1]
    values32 = lax.all_gather(flat, "tensor", axis=1, tiled=True).astype(jnp.float32)
    scaled = (values32 * final_gain[None, :]).astype(jnp.bfloat16)
    key_sum = jnp.dot(scaled, cross_key, preferred_element_type=jnp.float32)
    value_sum = jnp.dot(scaled, cross_value, preferred_element_type=jnp.float32)
    squares = jnp.sum(values32 * values32, axis=1, keepdims=True)
    key_sum, value_sum, squares = (key_sum, value_sum, squares)
    key_scale = lax.rsqrt(squares / width + EPSILON)
    grid_shape = (groups, slots, BLOCK, inner)
    key_grid = (key_sum * key_scale).astype(jnp.bfloat16).reshape(grid_shape)
    value_grid = (value_sum * key_scale).astype(jnp.bfloat16).reshape(grid_shape)
    key_ids = meta[:, :, 0]
    key_live = meta[:, :, 1]
    key_valid = position[None, None, :] < key_live[:, :, None]
    query_rows = decoder_states.shape[0]
    dec_normed = (
        decoder_states.astype(jnp.float32) * row_scale(decoder_states) * dec_gain[None, :]
    ).astype(jnp.bfloat16)
    cross_queries = jnp.dot(dec_normed, cross_query, preferred_element_type=jnp.float32).astype(
        jnp.bfloat16
    )
    allowed = (query_protein[:, None, None, None] == key_ids[None, :, :, None]) & key_valid[None]
    slot_total = groups * slots
    inner_width = key_grid.shape[3]
    cross_context = attend(
        cross_queries,
        key_grid.reshape(slot_total * BLOCK, inner_width),
        value_grid.reshape(slot_total * BLOCK, inner_width),
        allowed.reshape(query_rows, slot_total * BLOCK),
    )
    share_rows = query_rows // tensor_count
    mixed = summed_on_arrival(
        jnp.dot(cross_context, cross_out, preferred_element_type=jnp.float32).astype(jnp.bfloat16),
        "tensor",
        0,
    )
    own_rows = lax.dynamic_slice_in_dim(decoder_states, tensor_index * share_rows, share_rows, 0)
    decoded = (own_rows.astype(jnp.float32) + mixed).astype(jnp.bfloat16)
    return (encoded, decoded)


def solution(mesh):
    in_specs = (
        P("dp", None),
        P("dp"),
        P(),
        P(),
        P(),
        P(None, "tensor"),
        P(None, "tensor"),
        P(None, "tensor"),
        P("tensor", None),
        P("dp", None),
        P("dp"),
        P(),
        P(),
        P(None, "tensor"),
        P(None, "tensor"),
        P(None, "tensor"),
        P("tensor", None),
    )
    out_specs = (P("dp", "tensor"), P(("dp", "tensor"), None))
    return jax.shard_map(body, mesh=mesh, in_specs=in_specs, out_specs=out_specs, check_vma=False)
```

profile of v0, /device:TPU:0, one launch (start us, length us, event | category | flops | bytes accessed | tf_op | source)
XLA Modules:
  0.0 220.1 jit_solution(1068523723538875895)
XLA Ops:
  7.2 1.0 convert_reduce_fusion.2
  8.9 0.9 select_reduce_fusion.2
  10.1 1.5 fusion.17
  11.6 4.4 %fusion.31 = bf16[64,8,8,128]{3,2,1,0:T(8,128)(2,1)} fusion(bf16[1024,1024]{1,0:T(8,128)(2,1)} %param.22, bf16[512,1024]{1,0:T(8,128)(2,1)} %param.17, f32[1024]{0:T(1024)} %param.21, f32[512]{0:T(512)S(1)} %add_rsqrt_fusion.2), kind=kOutput, calls=%fused_computation.46 | convolution fusion | flops 1076363264 | bytes 4200448 | tf_op jit(solution)/shard_map/dot_general | solution.py:95
  16.0 2.3 %fusion.32 = bf16[64,8,8,128]{3,2,1,0:T(8,128)(2,1)} fusion(bf16[1024,1024]{1,0:T(8,128)(2,1)S(1)} %copy-done.11, bf16[512,1024]{1,0:T(8,128)(2,1)S(1)} %copy-done.6, f32[1024]{0:T(1024)S(1)} %copy-done.14, f32[512]{0:T(512)S(1)} %add_rsqrt_fusion.2), kind=kOutput, calls=%fused_computation.47 | convolution fusion | flops 1076363264 | bytes 4200448 | tf_op jit(solution)/shard_map/dot_general | solution.py:98
  18.3 2.3 %convolution_convert_fusion.3 = bf16[512,1024]{1,0:T(8,128)(2,1)} fusion(bf16[1024,1024]{1,0:T(8,128)(2,1)S(1)} %copy-done.12, bf16[512,1024]{1,0:T(8,128)(2,1)S(1)} %copy-done.6, f32[1024]{0:T(1024)S(1)} %copy-done.14, f32[512]{0:T(512)S(1)} %add_rsqrt_fusion.2), kind=kOutput, calls=%fused_computation.43 | convolution fusion | flops 1076363264 | bytes 4200448 | tf_op jit(solution)/shard_map/dot_general | solution.py:99
  20.6 2.3 %copy.107 = bf16[512,1024]{0,1:T(8,128)(2,1)} copy(bf16[512,1024]{1,0:T(8,128)(2,1)} %convolution_convert_fusion.3) | data formatting | bytes 2097152 | tf_op jit(solution)/shard_map/while/body/eval_jaxpr/reshape | solution.py:44
  22.9 4.0 %copy.91 = bf16[1024,1024]{0,1:T(8,128)(2,1)} copy(bf16[1024,1024]{1,0:T(8,128)(2,1)} %param.25) | data formatting | bytes 4194304 | tf_op args[8]
  27.1 3.2 %fusion.8 = (f32[8,512]{1,0:T(8,128)S(1)}, f32[8,512,512]{1,2,0:T(8,128)S(1)}) fusion(pred[512,512]{0,1:T(8,128)(4,1)S(1)} %compare_and_fusion, bf16[64,8,8,128]{3,2,1,0:T(8,128)(2,1)} %fusion.32, bf16[64,8,8,128]{3,2,1,0:T(8,128)(2,1)} %fusion.31), kind=kOutput, calls=%fused_computation.16 | convolution fusion | flops 543158272 | bytes 10764288 | tf_op jit(solution)/shard_map/while/body/eval_jaxpr/qhd,khd->hqk/dot_general | solution.py:45
  30.3 1.7 fusion.9
  32.1 2.6 %fusion.20 = bf16[512,8,128]{0,2,1:T(8,128)(2,1)S(1)} fusion(bf16[512,8,128]{0,2,1:T(8,128)(2,1)S(1)} %bitcast.70, f32[8,512,512]{1,2,0:T(8,128)S(1)} %get-tuple-element.33, f32[8,512]{1,0:T(8,128)S(1)} %get-tuple-element.32, pred[512,512]{0,1:T(8,128)(4,1)S(1)} %compare_and_fusion, f32[512,8]{0,1:T(8,128)S(1)} %bitcast.72), kind=kOutput, calls=%fused_computation.31 | convolution fusion | flops 546308096 | bytes 10780672 | tf_op jit(solution)/shard_map/while/body/eval_jaxpr/hqk,khd->qhd/dot_general | solution.py:53
  34.7 2.5 %convolution_bitcast_fusion = f32[16,512,64]{1,2,0:T(8,128)} fusion(bf16[512,1024,1]{0,1,2:T(8,128)(2,1)S(1)} %bitcast.77, bf16[16,64,1024]{2,1,0:T(8,128)(2,1)S(1)} %bitcast.69), kind=kOutput, calls=%fused_computation.34 | convolution fusion | flops 1073741824 | bytes 5242880 | tf_op jit(solution)/shard_map/dot_general | solution.py:116
  37.2 7.2 %all-to-all-start = ((f32[16,512,64]{1,2,0:T(8,128)}), f32[16,512,64]{1,2,0:T(8,128)}, u32[]{:S(2)}, u32[]{:S(2)}) async-start(f32[16,512,64]{1,2,0:T(8,128)} %convolution_bitcast_fusion), calls=%async_computation | async-start | bytes 4194304 | tf_op jit(solution)/shard_map/all_to_all | solution.py:19
  44.7 31.5 %all-to-all-done = f32[16,512,64]{1,2,0:T(8,128)} async-done(((f32[16,512,64]{1,2,0:T(8,128)}), f32[16,512,64]{1,2,0:T(8,128)}, u32[]{:S(2)}, u32[]{:S(2)}) %all-to-all-start) | async-done | bytes 2097184 | tf_op jit(solution)/shard_map/all_to_all | solution.py:19
  76.2 1.8 reduce_sum.122
  79.4 12.7 %all_to_all.20 = bf16[8,2,128,64]{2,3,1,0:T(8,128)(2,1)S(1)} all-to-all(bf16[8,2,128,64]{2,3,1,0:T(8,128)(2,1)S(1)} %copy.94), channel_id=1, replica_groups=mesh['dp'=8,'tensor'=16] {'dp'}, dimensions={0} | all-to-all | bytes 524288 | tf_op jit(solution)/shard_map/all_to_all | solution.py:138
  94.3 3.5 %all-to-all-start.2 = ((s32[8,2,2]{1,2,0:T(2,128)}), s32[8,2,2]{1,2,0:T(2,128)S(1)}, u32[]{:S(2)}, u32[]{:S(2)}) async-start(s32[8,2,2]{1,2,0:T(2,128)} %copy.96), calls=%async_computation.2 | async-start | bytes 16384 | tf_op jit(solution)/shard_map/all_to_all | solution.py:145
  97.8 1.4 fusion.25
  99.2 3.9 %fusion.33 = bf16[48,8,8,128]{3,2,1,0:T(8,128)(2,1)} fusion(bf16[1024,1024]{1,0:T(8,128)(2,1)} %param.30, bf16[384,1024]{1,0:T(8,128)(2,1)} %param.26, f32[1024]{0:T(1024)S(1)} %copy-done.15, f32[384]{0:T(512)S(1)} %add_rsqrt_fusion.1), kind=kOutput, calls=%fused_computation.48 | convolution fusion | flops 807272448 | bytes 3675648 | tf_op jit(solution)/shard_map/dot_general | solution.py:165
  103.3 1.3 bitcast_and_fusion
  104.6 2.2 copy.101
  106.8 33.9 %all-gather.2.cloned.1.call-done = bf16[2048,1024]{0,1:T(8,128)(2,1)} async-done(((bf16[2048,64]{0,1:T(8,128)(2,1)}), bf16[2048,1024]{0,1:T(8,128)(2,1)}) %all-gather.2.cloned.1.call-update) | async-done | bytes 4194320 | tf_op jit(solution)/shard_map/all_gather | solution.py:148
  140.7 3.2 %fusion.7 = f32[2048]{0:T(1024)S(1)} fusion(bf16[2048,1024]{0,1:T(8,128)(2,1)} %all-gather.2.cloned.1.call-done), kind=kLoop, calls=%fused_computation.11 | loop fusion | flops 6289408 | bytes 4202496 | tf_op jit(solution)/shard_map/reduce_sum | solution.py:152
  144.1 5.6 %multiply_convert_fusion = bf16[2048,1024]{0,1:T(8,128)(2,1)S(1)} fusion(bf16[1024,1024]{1,0:T(8,128)(2,1)S(1)} %copy-done, f32[2048]{0:T(1024)S(1)} %add_rsqrt_fusion, bf16[2048,1024]{0,1:T(8,128)(2,1)S(1)} %copy-done.2, f32[1024]{0:T(1024)S(1)} %copy-done.16), kind=kOutput, calls=%fused_computation.12 | convolution fusion | flops 4305453056 | bytes 10498048 | tf_op jit(solution)/shard_map/dot_general | solution.py:150
  149.8 10.9 %fusion = (f32[8,384]{1,0:T(8,128)S(1)}, f32[8,384,2048]{2,1,0:T(8,128)}) fusion(pred[384,2048]{1,0:T(8,128)(4,1)S(1)} %copy.101, bf16[2048,8,128]{0,2,1:T(8,128)(2,1)S(1)} %bitcast.68, bf16[48,8,8,128]{3,2,1,0:T(8,128)(2,1)S(1)} %copy-done.5), kind=kOutput, calls=%fused_computation.2 | convolution fusion | flops 1629484032 | bytes 30945280 | tf_op jit(solution)/shard_map/qhd,khd->hqk/dot_general | solution.py:45
  160.7 11.7 %fusion.1 = f32[8,384]{1,0:T(8,128)S(1)} fusion(f32[8,384,2048]{2,1,0:T(8,128)} %get-tuple-element.35, f32[8,384]{1,0:T(8,128)S(1)} %get-tuple-element.34, pred[384,2048]{1,0:T(8,128)(4,1)S(1)} %copy.101), kind=kLoop, calls=%fused_computation.3 | loop fusion | flops 25162752 | bytes 25976832 | tf_op jit(solution)/shard_map/reduce_sum | solution.py:51
  172.4 5.6 %multiply_convert_fusion.1 = bf16[2048,1024]{0,1:T(8,128)(2,1)S(1)} fusion(bf16[1024,1024]{1,0:T(8,128)(2,1)S(1)} %copy-done.13, f32[2048]{0:T(1024)S(1)} %add_rsqrt_fusion, bf16[2048,1024]{0,1:T(8,128)(2,1)S(1)} %copy-done.2, f32[1024]{0:T(1024)S(1)} %copy-done.16), kind=kOutput, calls=%fused_computation.13 | convolution fusion | flops 4305453056 | bytes 10498048 | tf_op jit(solution)/shard_map/dot_general | solution.py:151
  178.1 12.2 %fusion.28 = bf16[384,8,128]{0,2,1:T(8,128)(2,1)S(1)} fusion(bf16[2048,8,128]{0,2,1:T(8,128)(2,1)S(1)} %bitcast.76, f32[8,384,2048]{2,1,0:T(8,128)} %get-tuple-element.35, f32[8,384]{1,0:T(8,128)S(1)} %get-tuple-element.34, pred[384,2048]{1,0:T(8,128)(4,1)S(1)} %copy.101, f32[384,8]{0,1:T(8,128)S(1)} %bitcast.75), kind=kOutput, calls=%fused_computation.39 | convolution fusion | flops 1636564992 | bytes 30957568 | tf_op jit(solution)/shard_map/hqk,khd->qhd/dot_general | solution.py:53
  190.3 1.9 convolution_convert_fusion.4
  192.1 5.3 %all-to-all-start.3 = ((bf16[16,24,1024]{2,1,0:T(8,128)(2,1)}), bf16[16,24,1024]{2,1,0:T(8,128)(2,1)S(1)}, u32[]{:S(2)}, u32[]{:S(2)}) async-start(bf16[16,24,1024]{2,1,0:T(8,128)(2,1)} %bitcast.18), calls=%async_computation.3 | async-start | bytes 1572864 | tf_op jit(solution)/shard_map/all_to_all | solution.py:25
  197.4 14.3 %all-to-all-done.3 = bf16[16,24,1024]{2,1,0:T(8,128)(2,1)S(1)} async-done(((bf16[16,24,1024]{2,1,0:T(8,128)(2,1)}), bf16[16,24,1024]{2,1,0:T(8,128)(2,1)S(1)}, u32[]{:S(2)}, u32[]{:S(2)}) %all-to-all-start.3) | async-done | bytes 786464 | tf_op jit(solution)/shard_map/all_to_all | solution.py:25
  211.8 1.4 add_convert_fusion.1
  (67 shorter events, 5.6 us)
Async XLA Ops:
  7.2 136.7 %copy-start = (bf16[1024,1024]{1,0:T(8,128)(2,1)S(1)}, bf16[1024,1024]{1,0:T(8,128)(2,1)}, u32[]{:S(2)}) copy-start(bf16[1024,1024]{1,0:T(8,128)(2,1)} %param.31) | copy-start | bytes 6291460
  11.6 4.4 %copy-start.6 = (bf16[512,1024]{1,0:T(8,128)(2,1)S(1)}, bf16[512,1024]{1,0:T(8,128)(2,1)}, u32[]{:S(2)}) copy-start(bf16[512,1024]{1,0:T(8,128)(2,1)} %param.17) | copy-start | bytes 3145732
  11.6 4.4 %copy-start.11 = (bf16[1024,1024]{1,0:T(8,128)(2,1)S(1)}, bf16[1024,1024]{1,0:T(8,128)(2,1)}, u32[]{:S(2)}) copy-start(bf16[1024,1024]{1,0:T(8,128)(2,1)} %param.23) | copy-start | bytes 6291460
  11.6 4.4 %copy-start.14 = (f32[1024]{0:T(1024)S(1)}, f32[1024]{0:T(1024)}, u32[]{:S(2)}) copy-start(f32[1024]{0:T(1024)} %param.21) | copy-start | bytes 12292
  16.0 2.3 %copy-start.12 = (bf16[1024,1024]{1,0:T(8,128)(2,1)S(1)}, bf16[1024,1024]{1,0:T(8,128)(2,1)}, u32[]{:S(2)}) copy-start(bf16[1024,1024]{1,0:T(8,128)(2,1)} %param.24) | copy-start | bytes 6291460
  30.3 1.8 copy-start.7
  32.1 2.6 %copy-start.4 = (bf16[1024,1024]{0,1:T(8,128)(2,1)S(1)}, bf16[1024,1024]{0,1:T(8,128)(2,1)}, u32[]{:S(2)}) copy-start(bf16[1024,1024]{0,1:T(8,128)(2,1)} %copy.91) | copy-start | bytes 6291460
  37.2 39.0 %all-to-all-start = ((f32[16,512,64]{1,2,0:T(8,128)}), f32[16,512,64]{1,2,0:T(8,128)}, u32[]{:S(2)}, u32[]{:S(2)}) async-start(f32[16,512,64]{1,2,0:T(8,128)} %convolution_bitcast_fusion), calls=%async_computation | async-start | bytes 4194304 | tf_op jit(solution)/shard_map/all_to_all | solution.py:19
  44.4 49.0 %copy-start.9 = (s32[4]{0:T(128)S(1)}, s32[4]{0:T(128)}, u32[]{:S(2)}) copy-start(s32[4]{0:T(128)} %param.18) | copy-start | bytes 52
  44.4 54.8 %copy-start.15 = (f32[1024]{0:T(1024)S(1)}, f32[1024]{0:T(1024)}, u32[]{:S(2)}) copy-start(f32[1024]{0:T(1024)} %param.28) | copy-start | bytes 12292
  44.4 96.2 %all-gather.2.cloned.1.call-start = ((), (), s32[]{:S(2)}) async-start(), calls=%async_computation.4 | async-start | bytes 4456448 | tf_op jit(solution)/shard_map/all_gather | solution.py:148
  78.0 25.0 %copy-start.8 = (bf16[512,64]{0,1:T(8,128)(2,1)}, bf16[512,64]{0,1:T(8,128)(2,1)S(1)}, u32[]{:S(2)}) copy-start(bf16[512,64]{0,1:T(8,128)(2,1)S(1)} %add_convert_fusion) | copy-start | bytes 196612
  92.4 10.8 %copy-start.10 = (s32[384]{0:T(512)S(1)}, s32[384]{0:T(512)}, u32[]{:S(2)}) copy-start(s32[384]{0:T(512)} %param.27) | copy-start | bytes 4612
  94.3 8.8 %all-to-all-start.2 = ((s32[8,2,2]{1,2,0:T(2,128)}), s32[8,2,2]{1,2,0:T(2,128)S(1)}, u32[]{:S(2)}, u32[]{:S(2)}) async-start(s32[8,2,2]{1,2,0:T(2,128)} %copy.96), calls=%async_computation.2 | async-start | bytes 16384 | tf_op jit(solution)/shard_map/all_to_all | solution.py:145
  103.1 40.9 %copy-start.16 = (f32[1024]{0:T(1024)S(1)}, f32[1024]{0:T(1024)}, u32[]{:S(2)}) copy-start(f32[1024]{0:T(1024)} %param.29) | copy-start | bytes 12292
  140.7 3.4 %copy-start.2 = (bf16[2048,1024]{0,1:T(8,128)(2,1)S(1)}, bf16[2048,1024]{0,1:T(8,128)(2,1)}, u32[]{:S(2)}) copy-start(bf16[2048,1024]{0,1:T(8,128)(2,1)} %all-gather.2.cloned.1.call-done) | copy-start | bytes 12582916
  144.1 5.6 %copy-start.5 = (bf16[48,8,8,128]{3,2,1,0:T(8,128)(2,1)S(1)}, bf16[48,8,8,128]{3,2,1,0:T(8,128)(2,1)}, u32[]{:S(2)}) copy-start(bf16[48,8,8,128]{3,2,1,0:T(8,128)(2,1)} %fusion.33) | copy-start | bytes 2359300
  160.7 11.7 %copy-start.13 = (bf16[1024,1024]{1,0:T(8,128)(2,1)S(1)}, bf16[1024,1024]{1,0:T(8,128)(2,1)}, u32[]{:S(2)}) copy-start(bf16[1024,1024]{1,0:T(8,128)(2,1)} %param.32) | copy-start | bytes 6291460
  178.0 12.2 %copy-start.3 = (bf16[1024,1024]{1,0:T(8,128)(2,1)S(1)}, bf16[1024,1024]{1,0:T(8,128)(2,1)}, u32[]{:S(2)}) copy-start(bf16[1024,1024]{1,0:T(8,128)(2,1)} %param.33) | copy-start | bytes 6291460
  178.1 35.2 %copy-start.1 = (bf16[1024,1024]{1,0:T(8,128)(2,1)S(1)}, bf16[1024,1024]{1,0:T(8,128)(2,1)}, u32[]{:S(2)}) copy-start(bf16[1024,1024]{1,0:T(8,128)(2,1)} %param.31) | copy-start | bytes 6291460
  192.1 19.6 %all-to-all-start.3 = ((bf16[16,24,1024]{2,1,0:T(8,128)(2,1)}), bf16[16,24,1024]{2,1,0:T(8,128)(2,1)S(1)}, u32[]{:S(2)}, u32[]{:S(2)}) async-start(bf16[16,24,1024]{2,1,0:T(8,128)(2,1)} %bitcast.18), calls=%async_computation.3 | async-start | bytes 1572864 | tf_op jit(solution)/shard_map/all_to_all | solution.py:25
Sparse Core Ops, SparseCore 0:
  93.4 47.2 all-gather.1
where the time goes:
time: 221 us; the launch traced here: 220 us
  waiting for transfers between devices  79.8 us (36%)
  matrix products  57.7 us (26%)
  other arithmetic  27 us (12%)
  starting transfers between devices  16 us (7%)
  between operations  14.4 us (7%)
  blocking collectives  12.7 us (6%)
  local copies, waits for them, and re-layouts  12.6 us (6%)
    all_gather x1, waiting for transfers between devices, body(): lax.all_gather(flat, 'tensor', axis=1, tiled=True).astype(jnp.float32)  33.9 us
    all_to_all x1, waiting for transfers between devices, sent_and_summed(): lax.all_to_all(blocks, axis, split_axis=0, concat_axis=0, tiled=True)  31.5 us
    dot_general x2, matrix products, attend(): jnp.einsum('hqk,khd->qhd', weights, value_heads, preferred_element_type=j...  14.7 us
    all_to_all x1, waiting for transfers between devices, summed_on_arrival(): lax.all_to_all(blocks, axis, split_axis=0, concat_axis=0, tiled=True)  14.3 us
    dot_general x2, matrix products, attend(): jnp.einsum('qhd,khd->hqk', query_heads, key_heads, preferred_element_type...  14.1 us
    reduce_sum x2, other arithmetic, attend(): total = jnp.sum(expo, axis=2)  13.4 us
    all_to_all x1, blocking collectives, body(): lax.all_to_all(placed.reshape(groups, slots, BLOCK, features), 'dp', spli...  12.7 us
    all_to_all x1, starting transfers between devices, sent_and_summed(): lax.all_to_all(blocks, axis, split_axis=0, concat_axis=0, tiled=True)  7.19 us
  transfers between devices with their start and end apart: 4, of which 3 were waited for; matrix products, arithmetic and copies ran while one was open for 5% of the time, Pallas kernels for 0%

commit v1 on v0

--- a/solution.py
+++ b/solution.py
@@ -145,7 +145,9 @@
     meta = lax.all_to_all(send_meta, "dp", split_axis=0, concat_axis=0, tiled=True)
     flat = slice_grid.reshape(-1, slice_width)
     inner = cross_key.shape[1]
-    values32 = lax.all_gather(flat, "tensor", axis=1, tiled=True).astype(jnp.float32)
+    values32 = jnp.concatenate(
+        lax.all_to_all(jnp.stack([flat] * lax.axis_size("tensor")), "tensor", 0, 0), axis=1
+    ).astype(jnp.float32)
     scaled = (values32 * final_gain[None, :]).astype(jnp.bfloat16)
     key_sum = jnp.dot(scaled, cross_key, preferred_element_type=jnp.float32)
     value_sum = jnp.dot(scaled, cross_value, preferred_element_type=jnp.float32)

time: 221 us -> 240 us (1.086)
  waiting for transfers between devices: 79.8 us -> 112 us
  between operations: 14.4 us -> 1.01 us
  blocking collectives: 12.7 us -> 0 us
  starting transfers between devices: 16 us -> 25.6 us
    all_to_all x0 -> x2, waiting for transfers between devices: none -> 62.7 us  [the longest x1 56 us: body(): lax.all_to_all(jnp.stack([flat] * lax.axis_size('tensor')), 'tensor', 0, 0)]
    all_gather x1 -> x0, waiting for transfers between devices: 33.9 us -> none  [body(): lax.all_gather(flat, 'tensor', axis=1, tiled=True).astype(jnp.float32)]
    all_to_all x1 -> x0, blocking collectives: 12.7 us -> none  [body(): lax.all_to_all(placed.reshape(groups, slots, BLOCK, features), 'dp', spli...]
    all_to_all x0 -> x2, starting transfers between devices: none -> 9.97 us  [the longest x1 5.3 us: body(): lax.all_to_all(placed.reshape(groups, slots, BLOCK, features), 'dp', spli...]
    all_to_all x1, waiting for transfers between devices: 0.01 us -> 4.77 us  [body(): lax.all_to_all(send_meta, 'dp', split_axis=0, concat_axis=0, tiled=True)]
    convert_element_type x0 -> x1, other arithmetic: none -> 2.93 us  [body(): scaled = (values32 * final_gain[None, :]).astype(jnp.bfloat16)]
    another operation x0 -> x2, local copies, waits for them, and re-layouts: none -> 2.68 us  [body(): jnp.stack([flat] * lax.axis_size('tensor'))]
  transfers between devices with their start and end apart: 4 -> 5, of which waited for: 3 -> 5; matrix products, arithmetic and copies ran while one was open for 5% -> 4% of each run, Pallas kernels for 0% -> 0%
where the time goes in v1:
time: 240 us; the launch traced here: 239 us
  waiting for transfers between devices  112 us (47%)
  matrix products  56.2 us (23%)
  other arithmetic  28.4 us (12%)
  starting transfers between devices  25.6 us (11%)
  local copies, waits for them, and re-layouts  14.9 us (6%)
    all_to_all x1, waiting for transfers between devices, body(): lax.all_to_all(jnp.stack([flat] * lax.axis_size('tensor')), 'tensor', 0, 0)  56 us
    all_to_all x1, waiting for transfers between devices, sent_and_summed(): lax.all_to_all(blocks, axis, split_axis=0, concat_axis=0, tiled=True)  31.4 us
    dot_general x2, matrix products, attend(): jnp.einsum('hqk,khd->qhd', weights, value_heads, preferred_element_type=j...  14.6 us
    dot_general x2, matrix products, attend(): jnp.einsum('qhd,khd->hqk', query_heads, key_heads, preferred_element_type...  14.1 us
    all_to_all x1, waiting for transfers between devices, summed_on_arrival(): lax.all_to_all(blocks, axis, split_axis=0, concat_axis=0, tiled=True)  13.5 us
    reduce_sum x2, other arithmetic, attend(): total = jnp.sum(expo, axis=2)  13.3 us
    all_to_all x1, starting transfers between devices, sent_and_summed(): lax.all_to_all(blocks, axis, split_axis=0, concat_axis=0, tiled=True)  7.35 us
    all_to_all x1, waiting for transfers between devices, body(): lax.all_to_all(placed.reshape(groups, slots, BLOCK, features), 'dp', spli...  6.72 us
  transfers between devices with their start and end apart: 5, of which 5 were waited for; matrix products, arithmetic and copies ran while one was open for 4% of the time, Pallas kernels for 0%

profile of v1, /device:TPU:0, one launch (start us, length us, event | category | flops | bytes accessed | tf_op | source)
XLA Modules:
  0.0 238.6 jit_solution(3362723099648566507)
XLA Ops:
  3.5 1.5 fusion.16
  5.1 4.4 %fusion.28 = bf16[64,8,8,128]{3,2,1,0:T(8,128)(2,1)} fusion(bf16[1024,1024]{1,0:T(8,128)(2,1)} %param.22, bf16[512,1024]{1,0:T(8,128)(2,1)} %param.17, f32[1024]{0:T(1024)} %param.21, f32[512]{0:T(512)S(1)} %add_rsqrt_fusion.2), kind=kOutput, calls=%fused_computation.45 | convolution fusion | flops 1076363264 | bytes 4200448 | tf_op jit(solution)/shard_map/dot_general | solution.py:95
  9.5 2.3 fusion.29
  11.8 2.3 convolution_convert_fusion.3
  14.1 2.3 copy.108
  16.4 4.0 %copy.92 = bf16[1024,1024]{0,1:T(8,128)(2,1)} copy(bf16[1024,1024]{1,0:T(8,128)(2,1)} %param.25) | data formatting | bytes 4194304 | tf_op args[8]
  20.6 3.2 %fusion.7 = (f32[8,512]{1,0:T(8,128)S(1)}, f32[8,512,512]{1,2,0:T(8,128)S(1)}) fusion(pred[512,512]{0,1:T(8,128)(4,1)S(1)} %compare_and_fusion, bf16[64,8,8,128]{3,2,1,0:T(8,128)(2,1)} %fusion.29, bf16[64,8,8,128]{3,2,1,0:T(8,128)(2,1)} %fusion.28), kind=kOutput, calls=%fused_computation.15 | convolution fusion | flops 543158272 | bytes 10764288 | tf_op jit(solution)/shard_map/while/body/eval_jaxpr/qhd,khd->hqk/dot_general | solution.py:45
  23.8 1.7 fusion.8
  25.6 2.6 %fusion.19 = bf16[512,8,128]{0,2,1:T(8,128)(2,1)S(1)} fusion(bf16[512,8,128]{0,2,1:T(8,128)(2,1)S(1)} %bitcast.78, f32[8,512,512]{1,2,0:T(8,128)S(1)} %get-tuple-element.33, f32[8,512]{1,0:T(8,128)S(1)} %get-tuple-element.32, pred[512,512]{0,1:T(8,128)(4,1)S(1)} %compare_and_fusion, f32[512,8]{0,1:T(8,128)S(1)} %bitcast.80), kind=kOutput, calls=%fused_computation.30 | convolution fusion | flops 546308096 | bytes 10780672 | tf_op jit(solution)/shard_map/while/body/eval_jaxpr/hqk,khd->qhd/dot_general | solution.py:53
  28.1 2.5 %convolution_bitcast_fusion = f32[16,512,64]{1,2,0:T(8,128)} fusion(bf16[512,1024,1]{0,1,2:T(8,128)(2,1)S(1)} %bitcast.85, bf16[16,64,1024]{2,1,0:T(8,128)(2,1)S(1)} %bitcast.77), kind=kOutput, calls=%fused_computation.33 | convolution fusion | flops 1073741824 | bytes 5242880 | tf_op jit(solution)/shard_map/dot_general | solution.py:116
  30.7 7.3 %all-to-all-start = ((f32[16,512,64]{1,2,0:T(8,128)}), f32[16,512,64]{1,2,0:T(8,128)}, u32[]{:S(2)}, u32[]{:S(2)}) async-start(f32[16,512,64]{1,2,0:T(8,128)} %convolution_bitcast_fusion), calls=%async_computation | async-start | bytes 4194304 | tf_op jit(solution)/shard_map/all_to_all | solution.py:19
  38.4 31.4 %all-to-all-done = f32[16,512,64]{1,2,0:T(8,128)} async-done(((f32[16,512,64]{1,2,0:T(8,128)}), f32[16,512,64]{1,2,0:T(8,128)}, u32[]{:S(2)}, u32[]{:S(2)}) %all-to-all-start) | async-done | bytes 2097184 | tf_op jit(solution)/shard_map/all_to_all | solution.py:19
  69.9 1.8 reduce_sum.122
  73.7 5.3 %all-to-all-start.1 = ((bf16[8,2,128,64]{2,3,1,0:T(8,128)(2,1)}), bf16[8,2,128,64]{2,3,1,0:T(8,128)(2,1)S(1)}, u32[]{:S(2)}, u32[]{:S(2)}) async-start(bf16[8,2,128,64]{2,3,1,0:T(8,128)(2,1)} %copy.95), calls=%async_computation.1 | async-start | bytes 524288 | tf_op jit(solution)/shard_map/all_to_all | solution.py:138
  79.8 6.7 %all-to-all-done.1 = bf16[8,2,128,64]{2,3,1,0:T(8,128)(2,1)S(1)} async-done(((bf16[8,2,128,64]{2,3,1,0:T(8,128)(2,1)}), bf16[8,2,128,64]{2,3,1,0:T(8,128)(2,1)S(1)}, u32[]{:S(2)}, u32[]{:S(2)}) %all-to-all-start.1) | async-done | bytes 262176 | tf_op jit(solution)/shard_map/all_to_all | solution.py:138
  86.6 3.3 %all-to-all-start.3 = ((s32[8,2,2]{1,2,0:T(2,128)}), s32[8,2,2]{1,2,0:T(2,128)S(1)}, u32[]{:S(2)}, u32[]{:S(2)}) async-start(s32[8,2,2]{1,2,0:T(2,128)} %copy.97), calls=%async_computation.3 | async-start | bytes 16384 | tf_op jit(solution)/shard_map/all_to_all | solution.py:145
  90.4 4.8 %all-to-all-done.3 = s32[8,2,2]{1,2,0:T(2,128)S(1)} async-done(((s32[8,2,2]{1,2,0:T(2,128)}), s32[8,2,2]{1,2,0:T(2,128)S(1)}, u32[]{:S(2)}, u32[]{:S(2)}) %all-to-all-start.3) | async-done | bytes 160 | tf_op jit(solution)/shard_map/all_to_all | solution.py:145
  95.1 2.5 %stack.10 = bf16[16,2048,64]{1,2,0:T(8,128)(2,1)} broadcast(bf16[2048,64]{0,1:T(8,128)(2,1)S(1)} %stack_reshape.2), dimensions={1,2} | broadcast | bytes 4456448 | tf_op jit(solution)/shard_map/stack | solution.py:149
  97.6 4.7 %all-to-all-start.2 = ((bf16[16,2048,64]{1,2,0:T(8,128)(2,1)}), bf16[16,2048,64]{1,2,0:T(8,128)(2,1)}, u32[]{:S(2)}, u32[]{:S(2)}) async-start(bf16[16,2048,64]{1,2,0:T(8,128)(2,1)} %stack.10), calls=%async_computation.2 | async-start | bytes 8388608 | tf_op jit(solution)/shard_map/all_to_all | solution.py:149
  102.6 3.6 %fusion.30 = bf16[48,8,8,128]{3,2,1,0:T(8,128)(2,1)} fusion(bf16[1024,1024]{1,0:T(8,128)(2,1)} %param.30, bf16[384,1024]{1,0:T(8,128)(2,1)S(1)} %copy-done.7, f32[1024]{0:T(1024)S(1)} %copy-done.16, f32[384]{0:T(512)S(1)} %add_rsqrt_fusion.1), kind=kOutput, calls=%fused_computation.47 | convolution fusion | flops 807272448 | bytes 3675648 | tf_op jit(solution)/shard_map/dot_general | solution.py:167
  107.6 2.2 copy.102
  109.8 56.0 %all-to-all-done.2 = bf16[16,2048,64]{1,2,0:T(8,128)(2,1)} async-done(((bf16[16,2048,64]{1,2,0:T(8,128)(2,1)}), bf16[16,2048,64]{1,2,0:T(8,128)(2,1)}, u32[]{:S(2)}, u32[]{:S(2)}) %all-to-all-start.2) | async-done | bytes 4194336 | tf_op jit(solution)/shard_map/all_to_all | solution.py:149
  165.8 3.1 %multiply_reduce_fusion = f32[2048]{0:T(1024)S(1)} fusion(bf16[16,2048,64]{1,2,0:T(8,128)(2,1)} %all-to-all-done.2), kind=kLoop, calls=%fused_computation.12 | loop fusion | flops 6289408 | bytes 4202496 | tf_op jit(solution)/shard_map/reduce_sum | solution.py:154
  168.9 2.9 %fusion.6 = bf16[2048,1024]{0,1:T(8,128)(2,1)S(1)} fusion(f32[1024]{0:T(1024)S(1)} %copy-done.10, bf16[16,2048,64]{1,2,0:T(8,128)(2,1)} %all-to-all-done.2), kind=kLoop, calls=%fused_computation.9 | loop fusion | flops 6291456 | bytes 8392704 | tf_op jit(solution)/shard_map/convert_element_type | solution.py:151
  171.8 5.1 %multiply_convert_fusion = bf16[2048,1024]{0,1:T(8,128)(2,1)S(1)} fusion(bf16[2048,1024]{0,1:T(8,128)(2,1)S(1)} %fusion.6, bf16[1024,1024]{1,0:T(8,128)(2,1)S(1)} %copy-done, f32[2048]{0:T(1024)S(1)} %add_rsqrt_fusion), kind=kOutput, calls=%fused_computation.10 | convolution fusion | flops 4299161600 | bytes 10493952 | tf_op jit(solution)/shard_map/dot_general | solution.py:152
  176.9 5.1 %multiply_convert_fusion.1 = bf16[2048,1024]{0,1:T(8,128)(2,1)S(1)} fusion(bf16[2048,1024]{0,1:T(8,128)(2,1)S(1)} %fusion.6, bf16[1024,1024]{1,0:T(8,128)(2,1)S(1)} %copy-done.14, f32[2048]{0:T(1024)S(1)} %add_rsqrt_fusion), kind=kOutput, calls=%fused_computation.11 | convolution fusion | flops 4299161600 | bytes 10493952 | tf_op jit(solution)/shard_map/dot_general | solution.py:153
  182.0 10.9 %fusion = (f32[8,384]{1,0:T(8,128)S(1)}, f32[8,384,2048]{2,1,0:T(8,128)}) fusion(pred[384,2048]{1,0:T(8,128)(4,1)S(1)} %copy.102, bf16[2048,8,128]{0,2,1:T(8,128)(2,1)S(1)} %bitcast.76, bf16[48,8,8,128]{3,2,1,0:T(8,128)(2,1)S(1)} %copy-done.4), kind=kOutput, calls=%fused_computation.2 | convolution fusion | flops 1629484032 | bytes 30945280 | tf_op jit(solution)/shard_map/qhd,khd->hqk/dot_general | solution.py:45
  192.9 11.6 %fusion.1 = f32[8,384]{1,0:T(8,128)S(1)} fusion(f32[8,384,2048]{2,1,0:T(8,128)} %get-tuple-element.35, f32[8,384]{1,0:T(8,128)S(1)} %get-tuple-element.34, pred[384,2048]{1,0:T(8,128)(4,1)S(1)} %copy.102), kind=kLoop, calls=%fused_computation.3 | loop fusion | flops 25162752 | bytes 25976832 | tf_op jit(solution)/shard_map/reduce_sum | solution.py:51
  204.5 12.0 %fusion.25 = bf16[384,8,128]{0,2,1:T(8,128)(2,1)S(1)} fusion(bf16[2048,8,128]{0,2,1:T(8,128)(2,1)S(1)} %bitcast.84, f32[8,384,2048]{2,1,0:T(8,128)} %get-tuple-element.35, f32[8,384]{1,0:T(8,128)S(1)} %get-tuple-element.34, pred[384,2048]{1,0:T(8,128)(4,1)S(1)} %copy.102, f32[384,8]{0,1:T(8,128)S(1)} %bitcast.83), kind=kOutput, calls=%fused_computation.38 | convolution fusion | flops 1636564992 | bytes 30957568 | tf_op jit(solution)/shard_map/hqk,khd->qhd/dot_general | solution.py:53
  216.6 1.9 convolution_convert_fusion.4
  218.4 5.0 %all-to-all-start.4 = ((bf16[16,24,1024]{2,1,0:T(8,128)(2,1)}), bf16[16,24,1024]{2,1,0:T(8,128)(2,1)S(1)}, u32[]{:S(2)}, u32[]{:S(2)}) async-start(bf16[16,24,1024]{2,1,0:T(8,128)(2,1)} %bitcast.20), calls=%async_computation.4 | async-start | bytes 1572864 | tf_op jit(solution)/shard_map/all_to_all | solution.py:25
  223.5 13.5 %all-to-all-done.4 = bf16[16,24,1024]{2,1,0:T(8,128)(2,1)S(1)} async-done(((bf16[16,24,1024]{2,1,0:T(8,128)(2,1)}), bf16[16,24,1024]{2,1,0:T(8,128)(2,1)S(1)}, u32[]{:S(2)}, u32[]{:S(2)}) %all-to-all-start.4) | async-done | bytes 786464 | tf_op jit(solution)/shard_map/all_to_all | solution.py:25
  (69 shorter events, 10.2 us)
Async XLA Ops:
  0.6 171.2 %copy-start = (bf16[1024,1024]{1,0:T(8,128)(2,1)S(1)}, bf16[1024,1024]{1,0:T(8,128)(2,1)}, u32[]{:S(2)}) copy-start(bf16[1024,1024]{1,0:T(8,128)(2,1)} %param.31) | copy-start | bytes 6291460
  5.1 4.4 %copy-start.5 = (bf16[512,1024]{1,0:T(8,128)(2,1)S(1)}, bf16[512,1024]{1,0:T(8,128)(2,1)}, u32[]{:S(2)}) copy-start(bf16[512,1024]{1,0:T(8,128)(2,1)} %param.17) | copy-start | bytes 3145732
  5.1 4.4 %copy-start.12 = (bf16[1024,1024]{1,0:T(8,128)(2,1)S(1)}, bf16[1024,1024]{1,0:T(8,128)(2,1)}, u32[]{:S(2)}) copy-start(bf16[1024,1024]{1,0:T(8,128)(2,1)} %param.23) | copy-start | bytes 6291460
  5.1 4.4 %copy-start.15 = (f32[1024]{0:T(1024)S(1)}, f32[1024]{0:T(1024)}, u32[]{:S(2)}) copy-start(f32[1024]{0:T(1024)} %param.21) | copy-start | bytes 12292
  9.5 2.3 copy-start.13
  23.8 1.8 copy-start.6
  25.5 2.6 %copy-start.3 = (bf16[1024,1024]{0,1:T(8,128)(2,1)S(1)}, bf16[1024,1024]{0,1:T(8,128)(2,1)}, u32[]{:S(2)}) copy-start(bf16[1024,1024]{0,1:T(8,128)(2,1)} %copy.92) | copy-start | bytes 6291460
  30.7 7.7 %copy-start.9 = (s32[4]{0:T(128)S(1)}, s32[4]{0:T(128)}, u32[]{:S(2)}) copy-start(s32[4]{0:T(128)} %param.18) | copy-start | bytes 52
  30.7 39.2 %all-to-all-start = ((f32[16,512,64]{1,2,0:T(8,128)}), f32[16,512,64]{1,2,0:T(8,128)}, u32[]{:S(2)}, u32[]{:S(2)}) async-start(f32[16,512,64]{1,2,0:T(8,128)} %convolution_bitcast_fusion), calls=%async_computation | async-start | bytes 4194304 | tf_op jit(solution)/shard_map/all_to_all | solution.py:19
  71.6 26.0 %copy-start.8 = (bf16[512,64]{0,1:T(8,128)(2,1)}, bf16[512,64]{0,1:T(8,128)(2,1)S(1)}, u32[]{:S(2)}) copy-start(bf16[512,64]{0,1:T(8,128)(2,1)S(1)} %add_convert_fusion) | copy-start | bytes 196612
  73.7 12.8 %all-to-all-start.1 = ((bf16[8,2,128,64]{2,3,1,0:T(8,128)(2,1)}), bf16[8,2,128,64]{2,3,1,0:T(8,128)(2,1)S(1)}, u32[]{:S(2)}, u32[]{:S(2)}) async-start(bf16[8,2,128,64]{2,3,1,0:T(8,128)(2,1)} %copy.95), calls=%async_computation.1 | async-start | bytes 524288 | tf_op jit(solution)/shard_map/all_to_all | solution.py:138
  86.6 8.6 %all-to-all-start.3 = ((s32[8,2,2]{1,2,0:T(2,128)}), s32[8,2,2]{1,2,0:T(2,128)S(1)}, u32[]{:S(2)}, u32[]{:S(2)}) async-start(s32[8,2,2]{1,2,0:T(2,128)} %copy.97), calls=%async_computation.3 | async-start | bytes 16384 | tf_op jit(solution)/shard_map/all_to_all | solution.py:145
  97.6 4.7 %copy-start.7 = (bf16[384,1024]{1,0:T(8,128)(2,1)S(1)}, bf16[384,1024]{1,0:T(8,128)(2,1)}, u32[]{:S(2)}) copy-start(bf16[384,1024]{1,0:T(8,128)(2,1)} %param.26) | copy-start | bytes 2359300
  97.6 4.9 %copy-start.16 = (f32[1024]{0:T(1024)S(1)}, f32[1024]{0:T(1024)}, u32[]{:S(2)}) copy-start(f32[1024]{0:T(1024)} %param.28) | copy-start | bytes 12292
  97.6 68.1 %all-to-all-start.2 = ((bf16[16,2048,64]{1,2,0:T(8,128)(2,1)}), bf16[16,2048,64]{1,2,0:T(8,128)(2,1)}, u32[]{:S(2)}, u32[]{:S(2)}) async-start(bf16[16,2048,64]{1,2,0:T(8,128)(2,1)} %stack.10), calls=%async_computation.2 | async-start | bytes 8388608 | tf_op jit(solution)/shard_map/all_to_all | solution.py:149
  102.3 3.9 %copy-start.11 = (s32[384]{0:T(512)S(1)}, s32[384]{0:T(512)}, u32[]{:S(2)}) copy-start(s32[384]{0:T(512)} %param.27) | copy-start | bytes 4612
  106.1 62.7 %copy-start.10 = (f32[1024]{0:T(1024)S(1)}, f32[1024]{0:T(1024)}, u32[]{:S(2)}) copy-start(f32[1024]{0:T(1024)} %param.29) | copy-start | bytes 12292
  171.8 5.1 %copy-start.14 = (bf16[1024,1024]{1,0:T(8,128)(2,1)S(1)}, bf16[1024,1024]{1,0:T(8,128)(2,1)}, u32[]{:S(2)}) copy-start(bf16[1024,1024]{1,0:T(8,128)(2,1)} %param.32) | copy-start | bytes 6291460
  176.9 5.1 %copy-start.4 = (bf16[48,8,8,128]{3,2,1,0:T(8,128)(2,1)S(1)}, bf16[48,8,8,128]{3,2,1,0:T(8,128)(2,1)}, u32[]{:S(2)}) copy-start(bf16[48,8,8,128]{3,2,1,0:T(8,128)(2,1)} %fusion.30) | copy-start | bytes 2359300
  204.5 12.1 %copy-start.2 = (bf16[1024,1024]{1,0:T(8,128)(2,1)S(1)}, bf16[1024,1024]{1,0:T(8,128)(2,1)}, u32[]{:S(2)}) copy-start(bf16[1024,1024]{1,0:T(8,128)(2,1)} %param.33) | copy-start | bytes 6291460
  204.5 34.1 %copy-start.1 = (bf16[1024,1024]{1,0:T(8,128)(2,1)S(1)}, bf16[1024,1024]{1,0:T(8,128)(2,1)}, u32[]{:S(2)}) copy-start(bf16[1024,1024]{1,0:T(8,128)(2,1)} %param.31) | copy-start | bytes 6291460
  218.4 18.5 %all-to-all-start.4 = ((bf16[16,24,1024]{2,1,0:T(8,128)(2,1)}), bf16[16,24,1024]{2,1,0:T(8,128)(2,1)S(1)}, u32[]{:S(2)}, u32[]{:S(2)}) async-start(bf16[16,24,1024]{2,1,0:T(8,128)(2,1)} %bitcast.20), calls=%async_computation.4 | async-start | bytes 1572864 | tf_op jit(solution)/shard_map/all_to_all | solution.py:25
